TPU v7x, 32 devices: a whole 2x2x4 slice. The times are simulated.
32 devices in a mesh: groups: 2 (over x), inner: 16 (over z, y, core).
Axes of the slice: x: 2, y: 2, z: 4, core: 2. Of those that a mesh axis runs over, the one named last changes fastest.
Arguments:
- hidden_rows: bfloat16 [2048, 2048], P(('groups', 'inner')), parts along dimension 0, may hold values from -6 to 6
- token_embed: bfloat16 [2048, 2048], P(('groups', 'inner')), parts along dimension 0, may hold values from -6 to 6
- first_routes: int32 [2048, 8], P(('groups', 'inner')), parts along dimension 0, may hold values from 0 to 15, all different within a row; in each aligned block of 64 rows (0 to 63, 64 to 127, ...) at most 48 rows name the same one
- first_gates: float32 [2048, 8], P(('groups', 'inner')), parts along dimension 0, may hold values from 0.2 to 0.6
- first_gate_up: bfloat16 [16, 2048, 1024], P('inner'), may hold values from -0.125 to 0.125
- first_down: bfloat16 [16, 512, 2048], P('inner'), may hold values from -0.25 to 0.25
- second_routes: int32 [2048, 8], P(('groups', 'inner')), parts along dimension 0, may hold values from 0 to 15, all different within a row; in each aligned block of 64 rows (0 to 63, 64 to 127, ...) at most 48 rows name the same one
- second_gates: float32 [2048, 8], P(('groups', 'inner')), parts along dimension 0, may hold values from 0.2 to 0.6
- second_gate_up: bfloat16 [16, 2048, 1024], P('inner'), may hold values from -0.125 to 0.125
- second_down: bfloat16 [16, 512, 2048], P('inner'), may hold values from -0.25 to 0.25
- hidden_gain: float32 [2048], replicated, may hold values from 0.25 to 1.75
- embed_gain: float32 [2048], replicated, may hold values from 0.25 to 1.75
- merge_weight: bfloat16 [4096, 2048], P('inner'), may hold values from -0.09375 to 0.09375
Outputs:
- final_rows: bfloat16 [2048, 2048], P(('groups', 'inner')), parts along dimension 0
There are 2 independent parts, one for each index of `groups`. A program takes and returns all parts, laid end to end along the dimension named above; an argument that names none is the same for every part. Nothing has to cross between parts.
Inputs may be any that keep to these rules, and one draw needn't show every extreme that they name: `first_routes`: among the 64 tokens of one block, no expert is named more than 48 times, and in every draw some expert is named exactly 48 times in some block. `second_routes`: among the 64 tokens of one block, no expert is named more than 48 times, and in every draw some expert is named exactly 48 times in some block.
All inputs are finite; a program needn't handle non-finite values.
Results may differ from a plain program's by a relative error of at most 0.01.
Values may be sent and summed in bfloat16 or wider, within the bound.
A program may use at most 128 MiB of HBM per device.

v0:
```python
import jax
import jax.numpy as jnp
from jax import lax
from jax.sharding import PartitionSpec as P

EPSILON = 1e-06


def rms_scale(values, gain_vec):
    widened = values.astype(jnp.float32)
    inverse_rms = lax.rsqrt(jnp.mean(widened * widened, axis=-1, keepdims=True) + EPSILON)
    return (widened * inverse_rms * gain_vec).astype(jnp.bfloat16)


def dense_gates(routes, gates, experts):
    hit = routes[:, :, None] == jnp.arange(experts, dtype=jnp.int32)[None, None, :]
    return jnp.sum(jnp.where(hit, gates[:, :, None], 0.0), axis=1)


def dense_layer(rows, gate_column, gate_up, down):
    everyone = lax.all_gather(rows, "inner", axis=0, tiled=True)
    width = down.shape[0]
    projected = jnp.dot(everyone, gate_up, preferred_element_type=jnp.float32)
    inner = (jax.nn.silu(projected[:, :width]) * projected[:, width:]).astype(jnp.bfloat16)
    out = jnp.dot(inner, down, preferred_element_type=jnp.float32)
    share = jnp.where(gate_column > 0, out * gate_column, 0.0).astype(jnp.bfloat16)
    return lax.psum_scatter(share, "inner", scatter_dimension=0, tiled=True).astype(jnp.float32)


def local(
    hidden_rows,
    token_embed,
    first_routes,
    first_gates,
    first_gate_up,
    first_down,
    second_routes,
    second_gates,
    second_gate_up,
    second_down,
    hidden_gain,
    embed_gain,
    merge_weight,
):
    experts = lax.axis_size("inner")
    me = lax.axis_index("inner")
    both = jnp.concatenate(
        [
            dense_gates(first_routes, first_gates, experts),
            dense_gates(second_routes, second_gates, experts),
        ],
        axis=1,
    )
    both = lax.all_gather(both, "inner", axis=0, tiled=True)
    first_column = lax.dynamic_slice_in_dim(both, me, 1, axis=1)
    second_column = lax.dynamic_slice_in_dim(both, me + experts, 1, axis=1)

    first_moe = dense_layer(hidden_rows, first_column, first_gate_up[0], first_down[0])
    after_first = (hidden_rows.astype(jnp.float32) + first_moe).astype(jnp.bfloat16)
    merged_in = jnp.concatenate(
        [rms_scale(after_first, hidden_gain), rms_scale(token_embed, embed_gain)], axis=1
    )
    columns = lax.all_to_all(merged_in, "inner", split_axis=1, concat_axis=0, tiled=True)
    partial = jnp.dot(columns, merge_weight, preferred_element_type=jnp.float32)
    merged = lax.psum_scatter(
        partial.astype(jnp.bfloat16), "inner", scatter_dimension=0, tiled=True
    ).astype(jnp.float32)
    after_merge = (after_first.astype(jnp.float32) + jax.nn.silu(merged)).astype(jnp.bfloat16)
    second_moe = dense_layer(after_merge, second_column, second_gate_up[0], second_down[0])
    return (after_merge.astype(jnp.float32) + second_moe).astype(jnp.bfloat16)


def solution(mesh):
    rows = P(("groups", "inner"), None)
    return jax.shard_map(
        local,
        mesh=mesh,
        in_specs=(
            rows, rows, rows, rows,
            P("inner", None, None),
            P("inner", None, None),
            rows, rows,
            P("inner", None, None),
            P("inner", None, None),
            P(),
            P(),
            P("inner", None),
        ),
        out_specs=rows,
        check_vma=False,
    )
```

profile of v0, /device:TPU:0, one launch (start us, length us, event | category | flops | bytes accessed | tf_op | source)
XLA Modules:
  0.0 384.9 jit_solution(18183789587168572780)
XLA Ops:
  6.5 0.0 copy-start
  6.5 0.7 all-gather.4.cloned.1.call-update
  7.3 0.0 reduce-scatter.4.cloned.1.call-start
  7.3 0.8 select_reduce_fusion
  8.1 24.3 %all-gather = f32[16,64,32]{1,2,0:T(8,128)S(1)} all-gather(f32[1,64,32]{1,2,0:T(8,128)S(1)} %maximum_bitcast_fusion), channel_id=1, replica_groups=mesh['groups'=2,'inner'=16] {'inner'}, dimensions={0}, use_global_device_ids=true | all-gather | bytes 139264 | tf_op jit(solution)/shard_map/all_gather | solution.py:54
  32.3 0.2 copy.34
  32.5 0.1 reshape.26
  32.7 30.4 %all-gather.4.cloned.1.call-done = bf16[1024,2048]{1,0:T(8,128)(2,1)} async-done(((bf16[64,2048]{1,0:T(8,128)(2,1)}), bf16[1024,2048]{1,0:T(8,128)(2,1)}) %all-gather.4.cloned.1.call-update) | async-done | bytes 4194320 | tf_op jit(solution)/shard_map/all_gather | solution.py:21
  63.1 7.5 %fusion.2 = f32[1024,1024]{1,0:T(8,128)S(1)} fusion(bf16[1024,2048]{1,0:T(8,128)(2,1)} %all-gather.4.cloned.1.call-done, bf16[1,2048,1024]{2,1,0:T(8,128)(2,1)} %param.17), kind=kOutput, calls=%fused_computation.4 | convolution fusion | flops 4294967296 | bytes 12582912 | tf_op jit(solution)/shard_map/dot_general | solution.py:23
  70.6 4.1 %select_convert_fusion.1 = bf16[1024,2048]{1,0:T(8,128)(2,1)} fusion(f32[1024]{0:T(1024)S(1)} %bitcast.33, pred[1024]{0:T(1024)(128)(4,1)S(1)} %get-tuple-element.5, bf16[1,512,2048]{2,1,0:T(8,128)(2,1)S(1)} %copy-done, f32[1024,1024]{1,0:T(8,128)S(1)} %fusion.2), kind=kOutput, calls=%fused_computation.1 | convolution fusion | flops 2156920832 | bytes 10490880 | tf_op jit(solution)/shard_map/dot_general | solution.py:25
  74.7 0.0 reduce-scatter.4.cloned.1.call-update
  74.8 0.0 reduce-scatter.6.cloned.1.call-start
  74.8 0.9 copy-done.4
  75.7 0.2 fusion.12
  75.8 0.1 fusion.14
  76.0 70.2 %reduce-scatter.4.cloned.1.call-done = bf16[64,2048]{1,0:T(8,128)(2,1)} async-done(((bf16[1024,2048]{1,0:T(8,128)(2,1)}), bf16[64,2048]{1,0:T(8,128)(2,1)}) %reduce-scatter.4.cloned.1.call-update) | async-done | bytes 262160 | tf_op jit(solution)/shard_map/reduce_scatter | solution.py:27
  146.2 1.2 fusion.18
  147.5 1.1 fusion.20
  148.7 17.8 %all_to_all.19 = bf16[64,16,256]{2,0,1:T(8,128)(2,1)S(1)} all-to-all(bf16[64,16,256]{2,0,1:T(8,128)(2,1)S(1)} %bitcast.31), channel_id=1, replica_groups=mesh['groups'=2,'inner'=16] {'inner'}, dimensions={1} | all-to-all | bytes 1048576 | tf_op jit(solution)/shard_map/all_to_all | solution.py:63
  166.5 3.2 convolution_convert_fusion
  169.7 0.0 reduce-scatter.6.cloned.1.call-update
  169.7 0.0 all-gather.6.cloned.1.call-start
  169.7 72.4 %reduce-scatter.6.cloned.1.call-done = bf16[64,2048]{1,0:T(8,128)(2,1)} async-done(((bf16[1024,2048]{1,0:T(8,128)(2,1)}), bf16[64,2048]{1,0:T(8,128)(2,1)}) %reduce-scatter.6.cloned.1.call-update) | async-done | bytes 262160 | tf_op jit(solution)/shard_map/reduce_scatter | solution.py:65
  242.1 1.8 fusion.21
  244.0 0.0 all-gather.6.cloned.1.call-update
  244.0 0.0 reduce-scatter.8.cloned.1.call-start
  244.0 49.4 %all-gather.6.cloned.1.call-done = bf16[1024,2048]{1,0:T(8,128)(2,1)} async-done(((bf16[64,2048]{1,0:T(8,128)(2,1)}), bf16[1024,2048]{1,0:T(8,128)(2,1)}) %all-gather.6.cloned.1.call-update) | async-done | bytes 4194320 | tf_op jit(solution)/shard_map/all_gather | solution.py:21
  293.5 7.6 %fusion = f32[1024,1024]{1,0:T(8,128)S(1)} fusion(bf16[1024,2048]{1,0:T(8,128)(2,1)} %all-gather.6.cloned.1.call-done, bf16[1,2048,1024]{2,1,0:T(8,128)(2,1)} %param.21), kind=kOutput, calls=%fused_computation.2 | convolution fusion | flops 4294967296 | bytes 12582912 | tf_op jit(solution)/shard_map/dot_general | solution.py:23
  301.1 4.1 %select_convert_fusion = bf16[1024,2048]{1,0:T(8,128)(2,1)} fusion(f32[1024]{0:T(1024)S(1)} %bitcast.32, pred[1024]{0:T(1024)(128)(4,1)S(1)} %get-tuple-element.9, bf16[1,512,2048]{2,1,0:T(8,128)(2,1)S(1)} %copy-done.8, f32[1024,1024]{1,0:T(8,128)S(1)} %fusion), kind=kOutput, calls=%fused_computation | convolution fusion | flops 2156920832 | bytes 10490880 | tf_op jit(solution)/shard_map/dot_general | solution.py:25
  305.2 0.0 reduce-scatter.8.cloned.1.call-update
  305.2 71.4 %reduce-scatter.8.cloned.1.call-done = bf16[64,2048]{1,0:T(8,128)(2,1)} async-done(((bf16[1024,2048]{1,0:T(8,128)(2,1)}), bf16[64,2048]{1,0:T(8,128)(2,1)}) %reduce-scatter.8.cloned.1.call-update) | async-done | bytes 262160 | tf_op jit(solution)/shard_map/reduce_scatter | solution.py:27
  376.7 1.7 add_convert_fusion
  (23 shorter events, 0.2 us)
Async XLA Ops:
  6.5 64.1 %copy-start = (bf16[1,512,2048]{2,1,0:T(8,128)(2,1)S(1)}, bf16[1,512,2048]{2,1,0:T(8,128)(2,1)}, u32[]{:S(2)}) copy-start(bf16[1,512,2048]{2,1,0:T(8,128)(2,1)} %param.18) | copy-start | bytes 6291460
  6.5 56.6 %all-gather.4.cloned.1.call-start = ((), (), s32[]{:S(2)}) async-start(), calls=%async_computation.4 | async-start | bytes 4456448 | tf_op jit(solution)/shard_map/all_gather | solution.py:21
  7.3 139.0 %reduce-scatter.4.cloned.1.call-start = ((), (), s32[]{:S(2)}) async-start(), calls=%async_computation.5 | async-start | bytes 4456448 | tf_op jit(solution)/shard_map/reduce_scatter | solution.py:27
  74.7 0.9 copy-start.4
  74.7 1.1 copy-start.6
  74.7 71.5 %copy-start.1 = (bf16[64,2048]{1,0:T(8,128)(2,1)S(1)}, bf16[64,2048]{1,0:T(8,128)(2,1)}, u32[]{:S(2)}) copy-start(bf16[64,2048]{1,0:T(8,128)(2,1)} %param.13) | copy-start | bytes 786436
  74.7 72.7 %copy-start.7 = (f32[2048]{0:T(1024)S(1)}, f32[2048]{0:T(1024)}, u32[]{:S(2)}) copy-start(f32[2048]{0:T(1024)} %param.23) | copy-start | bytes 24580
  74.8 167.4 %reduce-scatter.6.cloned.1.call-start = ((), (), s32[]{:S(2)}) async-start(), calls=%async_computation.6 | async-start | bytes 4456448 | tf_op jit(solution)/shard_map/reduce_scatter | solution.py:65
  146.2 20.3 %copy-start.5 = (bf16[256,2048]{1,0:T(8,128)(2,1)S(1)}, bf16[256,2048]{1,0:T(8,128)(2,1)}, u32[]{:S(2)}) copy-start(bf16[256,2048]{1,0:T(8,128)(2,1)} %param.25) | copy-start | bytes 3145732
  166.5 75.6 %copy-start.3 = (bf16[64,2048]{1,0:T(8,128)(2,1)S(1)}, bf16[64,2048]{1,0:T(8,128)(2,1)}, u32[]{:S(2)}) copy-start(bf16[64,2048]{1,0:T(8,128)(2,1)} %reduce-scatter.4.cloned.1.call-done) | copy-start | bytes 786436
  169.7 123.8 %all-gather.6.cloned.1.call-start = ((), (), s32[]{:S(2)}) async-start(), calls=%async_computation.7 | async-start | bytes 4456448 | tf_op jit(solution)/shard_map/all_gather | solution.py:21
  244.0 132.7 %reduce-scatter.8.cloned.1.call-start = ((), (), s32[]{:S(2)}) async-start(), calls=%async_computation.8 | async-start | bytes 4456448 | tf_op jit(solution)/shard_map/reduce_scatter | solution.py:27
  293.5 7.7 %copy-start.8 = (bf16[1,512,2048]{2,1,0:T(8,128)(2,1)S(1)}, bf16[1,512,2048]{2,1,0:T(8,128)(2,1)}, u32[]{:S(2)}) copy-start(bf16[1,512,2048]{2,1,0:T(8,128)(2,1)} %param.22) | copy-start | bytes 6291460
  305.2 71.5 %copy-start.2 = (bf16[64,2048]{1,0:T(8,128)(2,1)S(1)}, bf16[64,2048]{1,0:T(8,128)(2,1)}, u32[]{:S(2)}) copy-start(bf16[64,2048]{1,0:T(8,128)(2,1)} %fusion.21) | copy-start | bytes 786436
Sparse Core Ops, SparseCore 0:
  9.5 53.5 all-gather.3
  74.9 71.2 reduce-scatter.3
  169.8 72.2 reduce-scatter.5
  244.1 49.2 all-gather.5
  305.4 71.2 reduce-scatter.7
where the time goes:
time: 385 us
  waiting for transfers between devices  295 us (77%)
  blocking collectives  42.1 us (11%)
  matrix products  26.5 us (7%)
  between operations  13.2 us (3%)
  other arithmetic  7.03 us (2%)
    reduce_scatter x2, waiting for transfers between devices, dense_layer(): lax.psum_scatter(share, 'inner', scatter_dimension=0, tiled=True)  142 us
    all_gather x2, waiting for transfers between devices, dense_layer(): everyone = lax.all_gather(rows, 'inner', axis=0, tiled=True)  79.8 us
    reduce_scatter x1, waiting for transfers between devices, local(): lax.psum_scatter(partial.astype(jnp.bfloat16), 'inner', scatter_dimension...  72.4 us
    all_gather x1, blocking collectives, local(): both = lax.all_gather(both, 'inner', axis=0, tiled=True)  24.3 us
    all_to_all x1, blocking collectives, local(): lax.all_to_all(merged_in, 'inner', split_axis=1, concat_axis=0, tiled=True)  17.8 us
    dot_general x2, matrix products, dense_layer(): projected = jnp.dot(everyone, gate_up, preferred_element_type=jnp.float32)  15.1 us
    dot_general x2, matrix products, dense_layer(): out = jnp.dot(inner, down, preferred_element_type=jnp.float32)  8.21 us
  transfers between devices with their start and end apart: 5, of which 5 were waited for; matrix products, arithmetic and copies ran while one was open for 0% of the time, Pallas kernels for 0%

commit v1 on v0

v1 whole, which is shorter than its diff:
```python
import functools

import jax
import jax.numpy as jnp
from jax import lax
from jax.experimental import pallas as pl
from jax.experimental.pallas import tpu as pltpu
from jax.sharding import PartitionSpec as P

EPSILON = 1e-06
LANES = 128
VMEM_LIMIT = 60 * 1024 * 1024


class Ring:
    def __init__(self, devices, tok):
        self.devices, self.tok = devices, tok
        self.chips = devices // 2
        self.reach = self.chips // 2
        self.rise = self.chips // 2
        me = lax.axis_index("inner")
        chip = me // 2
        across = chip % 2
        along = chip // 2
        self.core = me % 2
        self.place = along * (1 - across) + (2 * self.rise - 1 - along) * across
        self.me = me

    def device(self, shift, other):
        place = (self.place + shift + self.chips) % self.chips
        across = place // self.rise
        along = place * (1 - across) + (2 * self.rise - 1 - place) * across
        core = self.core * (1 - other) + (1 - self.core) * other
        return (along * 2 + across) * 2 + core

    def row(self, way, distance, other):
        if distance == 0:
            return ((self.reach - 1) * 4 + 2 + other) * self.tok
        if distance == self.reach:
            return ((self.reach - 1) * 4 + other) * self.tok
        return ((distance - 1) * 4 + way * 2 + other) * self.tok

    def half(self, way, distance, other, k):
        part = self.tok // 2
        return pl.ds(self.row(way, distance, other) + k * part, part)

    def block(self, way, distance, other):
        return pl.ds(self.row(way, distance, other), self.tok)


def remote(src, dst, send, recv, device):
    return pltpu.make_async_remote_copy(
        src_ref=src, dst_ref=dst, send_sem=send, recv_sem=recv,
        device_id={"inner": device}, device_id_type=pl.DeviceIdType.MESH,
    )


def greet(devices):
    barrier = pltpu.get_barrier_semaphore()
    for device in devices:
        pl.semaphore_signal(
            barrier, inc=1, device_id={"inner": device}, device_id_type=pl.DeviceIdType.MESH
        )
    pl.semaphore_wait(barrier, len(devices))


def wide(values):
    return values.astype(jnp.float32)


def narrow(values):
    return values.astype(jnp.bfloat16)


class Reduce:
    def __init__(self, ring, share, paired, arrived, sems):
        self.ring, self.share, self.paired, self.arrived = ring, share, paired, arrived
        self.pair_send, self.pair_recv, self.send, self.recv = sems
        self.started = []

    def slots(self, distance):
        return ((0,) if distance in (0, self.ring.reach) else (0, 1))

    def pair_copy(self, way, distance):
        ring = self.ring
        slot = ring.reach * 2 if distance == 0 else (distance - 1) * 2 + way
        here = self.paired.at[pl.ds(slot * ring.tok, ring.tok)]
        return remote(
            self.share.at[ring.block(way, distance, 1)], here,
            self.pair_send.at[slot], self.pair_recv.at[slot], ring.device(0, 1),
        ), here

    def start_pair(self, distance):
        for way in self.slots(distance):
            copy, _ = self.pair_copy(way, distance)
            copy.start()
            self.started.append(copy)

    def finish_pair(self, distance):
        for way in self.slots(distance):
            copy, here = self.pair_copy(way, distance)
            copy.wait_recv()
            rows = self.ring.block(way, distance, 0)
            self.share[rows, :] = narrow(wide(self.share[rows, :]) + wide(here[...]))

    def hop(self, way, distance, k):
        ring = self.ring
        part = ring.tok // 2
        slot = (way * ring.reach + distance - 1) * 2 + k
        landing = self.arrived.at[pl.ds(slot * part, part)]
        return remote(
            self.share.at[ring.half(1 - way, distance, 0, k)], landing,
            self.send.at[slot], self.recv.at[slot], ring.device(1 - 2 * way, 0),
        ), landing

    def start_hop(self, way, distance, k):
        copy, _ = self.hop(way, distance, k)
        copy.start()
        self.started.append(copy)

    def step(self, way, distance, k):
        copy, landing = self.hop(way, distance + 1, k)
        copy.wait_recv()
        rows = self.ring.half(1 - way, distance, 0, k)
        self.share[rows, :] = narrow(wide(self.share[rows, :]) + wide(landing[...]))
        self.start_hop(way, distance, k)

    def early(self):
        reach = self.ring.reach
        if reach > 1:
            for way in (0, 1):
                self.start_hop(way, reach - 1, 1 - way)

    def late(self):
        reach = self.ring.reach
        for way in (0, 1):
            self.start_hop(way, reach, way)

    def run(self, base, out):
        reach = self.ring.reach
        for distance in range(reach - 1, 0, -1):
            for way in (0, 1):
                self.step(way, distance, way)
            if distance > 1:
                for way in (0, 1):
                    self.step(way, distance - 1, 1 - way)
        part = self.ring.tok // 2
        for k in (0, 1):
            total = wide(self.share[self.ring.half(0, 0, 0, k), :])
            for way in (0, 1):
                if k == way or reach > 1:
                    copy, landing = self.hop(way, 1, k)
                    copy.wait_recv()
                    total = total + wide(landing[...])
            rows = pl.ds(k * part, part)
            out[rows, :] = base(rows, total)
        for copy in self.started:
            copy.wait_send()


def reduce_scratch(devices, tok, width):
    chips = devices // 2
    reach = chips // 2
    return [
        pltpu.VMEM((devices * tok, width), jnp.bfloat16),
        pltpu.VMEM(((2 * reach + 1) * tok, width), jnp.bfloat16),
        pltpu.VMEM((2 * reach * tok, width), jnp.bfloat16),
        pltpu.SemaphoreType.DMA((2 * reach + 1,)),
        pltpu.SemaphoreType.DMA((2 * reach + 1,)),
        pltpu.SemaphoreType.DMA((4 * reach,)),
        pltpu.SemaphoreType.DMA((4 * reach,)),
    ]


def layer_kernel(
    devices, x_ref, gu_ref, down_ref, out_ref, everyone, gu, down, inner,
    share, paired, arrived, pair_send, pair_recv, hop_send, hop_recv,
    load_sem, send, recv, sib_send, sib_recv,
):
    tok = x_ref.shape[0]
    width = out_ref.shape[1]
    hidden = down.shape[0]
    ring = Ring(devices, tok)
    reach = ring.reach
    part = tok // 2
    loads = [
        pltpu.make_async_copy(gu_ref.at[0], gu, load_sem.at[0]),
        pltpu.make_async_copy(down_ref.at[0], down, load_sem.at[1]),
    ]
    for load in loads:
        load.start()
    greet([ring.device(1, 0), ring.device(-1, 0), ring.device(0, 1)])
    started = []

    def ring_copy(way, distance, k):
        slot = (way * reach + distance - 1) * 2 + k
        landing = everyone.at[ring.half(way, distance, 0, k)]
        source = (
            x_ref.at[pl.ds(k * part, part)]
            if distance == 1
            else everyone.at[ring.half(way, distance - 1, 0, k)]
        )
        return remote(source, landing, send.at[slot], recv.at[slot], ring.device(1 - 2 * way, 0))

    def sibling_copy(way, distance, k):
        slot = 4 * reach if distance == 0 else (way * reach + distance - 1) * 2 + k
        if distance == 0:
            source, landing = x_ref, everyone.at[ring.block(0, 0, 1)]
        else:
            source = everyone.at[ring.half(way, distance, 0, k)]
            landing = everyone.at[ring.half(way, distance, 1, k)]
        return remote(source, landing, sib_send.at[slot], sib_recv.at[slot], ring.device(0, 1))

    def begin(copy):
        copy.start()
        started.append(copy)

    reducing = Reduce(ring, share, paired, arrived, (pair_send, pair_recv, hop_send, hop_recv))

    def compute(distance):
        rows = pl.ds((distance - 1) * 4 * tok, 4 * tok)
        x = everyone.at[rows]
        step = min(256, hidden)

        @pl.loop(0, hidden // step)
        def _(j):
            left = pl.ds(pl.multiple_of(j * step, step), step)
            right = pl.ds(pl.multiple_of(hidden + j * step, step), step)
            g = jnp.dot(x[:, :width], gu[:, left], preferred_element_type=jnp.float32)
            u = jnp.dot(x[:, :width], gu[:, right], preferred_element_type=jnp.float32)
            inner[:, left] = narrow(jax.nn.silu(g) * u)

        pad = x.shape[1] - width
        lane = lax.broadcasted_iota(jnp.int32, (4 * tok, pad), 1)
        mine = (lane == ring.me) | (lane == ring.me + devices)
        gate = jnp.sum(jnp.where(mine, wide(x[:, width:]), 0.0), axis=1, keepdims=True)
        span = min(512, width)

        @pl.loop(0, width // span)
        def _(j):
            columns = pl.ds(pl.multiple_of(j * span, span), span)
            out = jnp.dot(inner[...], down[:, columns], preferred_element_type=jnp.float32)
            share[rows, columns] = narrow(out * gate)

    for way in (0, 1):
        begin(ring_copy(way, 1, way))
    for way in (0, 1):
        if reach > 1:
            begin(ring_copy(way, 1, 1 - way))
    begin(sibling_copy(0, 0, 0))
    everyone[ring.block(0, 0, 0), :] = x_ref[...]

    def arrivals(distance):
        for short in (0, 1):
            for way in (0, 1):
                k = way if short == 0 else 1 - way
                if short and distance == reach:
                    continue
                ring_copy(way, distance, k).wait_recv()
                if distance < reach and not (short and distance == reach - 1):
                    begin(ring_copy(way, distance + 1, k))
                begin(sibling_copy(way, distance, k))

    def sibling_arrivals(distance):
        for short in (0, 1):
            for way in (0, 1):
                k = way if short == 0 else 1 - way
                if short and distance == reach:
                    continue
                sibling_copy(way, distance, k).wait_recv()

    for distance in range(1, reach + 1):
        arrivals(distance)
        if distance == 1:
            for load in loads:
                load.wait()
        else:
            sibling_arrivals(distance - 1)
            compute(distance - 1)
            reducing.start_pair(distance - 1)
    for distance in range(1, reach):
        reducing.finish_pair(distance)
    reducing.early()
    sibling_arrivals(reach)
    sibling_copy(0, 0, 0).wait_recv()
    compute(reach)
    reducing.start_pair(reach)
    reducing.start_pair(0)
    reducing.finish_pair(reach)
    reducing.late()
    reducing.finish_pair(0)
    reducing.run(lambda rows, total: narrow(wide(x_ref[rows, :width]) + total), out_ref)
    for copy in started:
        copy.wait_send()


def routed_layer(devices, number, rows, routes, gates, gate_up, down):
    tok, width = rows.shape
    reach = devices // 4
    dense = dense_gates(routes, gates, devices)
    high = narrow(dense)
    low = narrow(dense - wide(high))
    pad = -(-2 * devices // LANES) * LANES - 2 * devices
    packed = jnp.concatenate([rows, high, low, jnp.zeros((tok, pad), jnp.bfloat16)], axis=1)
    hidden = down.shape[1]
    vmem = pl.BlockSpec(memory_space=pltpu.VMEM)
    return pl.pallas_call(
        functools.partial(layer_kernel, devices),
        out_shape=jax.ShapeDtypeStruct((tok, width), jnp.bfloat16),
        in_specs=[vmem, pl.BlockSpec(memory_space=pl.ANY), pl.BlockSpec(memory_space=pl.ANY)],
        out_specs=vmem,
        scratch_shapes=[
            pltpu.VMEM((devices * tok, packed.shape[1]), jnp.bfloat16),
            pltpu.VMEM(gate_up.shape[1:], jnp.bfloat16),
            pltpu.VMEM(down.shape[1:], jnp.bfloat16),
            pltpu.VMEM((4 * tok, hidden), jnp.bfloat16),
        ]
        + reduce_scratch(devices, tok, width)
        + [
            pltpu.SemaphoreType.DMA((2,)),
            pltpu.SemaphoreType.DMA((4 * reach,)),
            pltpu.SemaphoreType.DMA((4 * reach,)),
            pltpu.SemaphoreType.DMA((4 * reach + 1,)),
            pltpu.SemaphoreType.DMA((4 * reach + 1,)),
        ],
        compiler_params=pltpu.CompilerParams(
            collective_id=number, has_side_effects=True, vmem_limit_bytes=VMEM_LIMIT
        ),
    )(packed, gate_up, down)


def merge_kernel(
    devices, pieces_ref, rows_ref, weight_ref, out_ref, columns,
    share, paired, arrived, pair_send, pair_recv, hop_send, hop_recv, send, recv, own_sem,
):
    tok, width = rows_ref.shape
    ring = Ring(devices, tok)
    reach = ring.reach
    partners = [(0, 0, 1)]
    for distance in range(1, reach + 1):
        for other in (0, 1):
            partners.append((0, distance, other))
            if distance < reach:
                partners.append((1, distance, other))

    def shift(way, distance):
        return distance * (1 - 2 * way)

    own = pltpu.make_async_copy(
        pieces_ref.at[ring.me], columns.at[ring.block(0, 0, 0)], own_sem
    )
    own.start()
    greet([ring.device(shift(way, distance), other) for way, distance, other in partners])

    def piece(way, distance, other):
        target = ring.device(shift(way, distance), other)
        slot = ring.row(way, distance, other) // tok
        landing = columns.at[ring.block(way, distance, other)]
        return remote(pieces_ref.at[target], landing, send.at[slot], recv.at[slot], target)

    sent = [piece(*partner) for partner in reversed(partners)]
    for copy in sent:
        copy.start()
    own.wait()
    reducing = Reduce(ring, share, paired, arrived, (pair_send, pair_recv, hop_send, hop_recv))

    def compute(distance):
        rows = pl.ds((distance - 1) * 4 * tok, 4 * tok)
        span = min(512, width)

        @pl.loop(0, width // span)
        def _(j):
            part = pl.ds(pl.multiple_of(j * span, span), span)
            share[rows, part] = narrow(
                jnp.dot(columns[rows, :], weight_ref[:, part], preferred_element_type=jnp.float32)
            )

    for distance in range(reach, 0, -1):
        for way, far, other in partners:
            if far == distance or (far == 0 and distance == reach):
                piece(way, far, other).wait_recv()
        compute(distance)
        reducing.start_pair(distance)
        if distance == reach:
            reducing.start_pair(0)
            reducing.finish_pair(reach)
            reducing.late()
            reducing.finish_pair(0)
        else:
            reducing.finish_pair(distance)
            if distance == reach - 1:
                reducing.early()
    reducing.run(
        lambda rows, total: narrow(wide(rows_ref[rows, :]) + jax.nn.silu(total)), out_ref
    )
    for copy in sent:
        copy.wait_send()


def merge(devices, number, after_first, merged_in, weight):
    tok, width = after_first.shape
    depth = weight.shape[0]
    pieces = merged_in.reshape(tok, devices, depth).transpose(1, 0, 2)
    vmem = pl.BlockSpec(memory_space=pltpu.VMEM)
    return pl.pallas_call(
        functools.partial(merge_kernel, devices),
        out_shape=jax.ShapeDtypeStruct((tok, width), jnp.bfloat16),
        in_specs=[vmem] * 3,
        out_specs=vmem,
        scratch_shapes=[pltpu.VMEM((devices * tok, depth), jnp.bfloat16)]
        + reduce_scratch(devices, tok, width)
        + [
            pltpu.SemaphoreType.DMA((devices,)),
            pltpu.SemaphoreType.DMA((devices,)),
            pltpu.SemaphoreType.DMA,
        ],
        compiler_params=pltpu.CompilerParams(
            collective_id=number, has_side_effects=True, vmem_limit_bytes=VMEM_LIMIT
        ),
    )(pieces, after_first, weight)


def rms_scale(values, gain_vec):
    widened = values.astype(jnp.float32)
    inverse_rms = lax.rsqrt(jnp.mean(widened * widened, axis=-1, keepdims=True) + EPSILON)
    return (widened * inverse_rms * gain_vec).astype(jnp.bfloat16)


def dense_gates(routes, gates, experts):
    hit = routes[:, :, None] == jnp.arange(experts, dtype=jnp.int32)[None, None, :]
    return jnp.sum(jnp.where(hit, gates[:, :, None], 0.0), axis=1)


def plain_layer(devices, rows, routes, gates, gate_up, down):
    dense = lax.all_gather(dense_gates(routes, gates, devices), "inner", axis=0, tiled=True)
    column = lax.dynamic_slice_in_dim(dense, lax.axis_index("inner"), 1, axis=1)
    everyone = lax.all_gather(rows, "inner", axis=0, tiled=True)
    width = down.shape[1]
    projected = jnp.dot(everyone, gate_up[0], preferred_element_type=jnp.float32)
    inner = narrow(jax.nn.silu(projected[:, :width]) * projected[:, width:])
    share = narrow(jnp.dot(inner, down[0], preferred_element_type=jnp.float32) * column)
    total = lax.psum_scatter(share, "inner", scatter_dimension=0, tiled=True)
    return narrow(wide(rows) + wide(total))


def plain_merge(after_first, merged_in, weight):
    columns = lax.all_to_all(merged_in, "inner", split_axis=1, concat_axis=0, tiled=True)
    partial = narrow(jnp.dot(columns, weight, preferred_element_type=jnp.float32))
    merged = lax.psum_scatter(partial, "inner", scatter_dimension=0, tiled=True)
    return narrow(wide(after_first) + jax.nn.silu(wide(merged)))


def local(
    hidden_rows,
    token_embed,
    first_routes,
    first_gates,
    first_gate_up,
    first_down,
    second_routes,
    second_gates,
    second_gate_up,
    second_down,
    hidden_gain,
    embed_gain,
    merge_weight,
):
    devices = lax.axis_size("inner")
    tok, width = hidden_rows.shape
    fits = 3 * devices * tok * width * 2 <= VMEM_LIMIT // 3 and devices % 4 == 0
    if fits:
        layer = lambda number, *operands: routed_layer(devices, number, *operands)
        join = functools.partial(merge, devices, 1)
    else:
        layer = lambda number, *operands: plain_layer(devices, *operands)
        join = plain_merge
    after_first = layer(0, hidden_rows, first_routes, first_gates, first_gate_up, first_down)
    merged_in = jnp.concatenate(
        [rms_scale(after_first, hidden_gain), rms_scale(token_embed, embed_gain)], axis=1
    )
    after_merge = join(after_first, merged_in, merge_weight)
    return layer(2, after_merge, second_routes, second_gates, second_gate_up, second_down)


def solution(mesh):
    rows = P(("groups", "inner"), None)
    return jax.shard_map(
        local,
        mesh=mesh,
        in_specs=(
            rows, rows, rows, rows,
            P("inner", None, None),
            P("inner", None, None),
            rows, rows,
            P("inner", None, None),
            P("inner", None, None),
            P(),
            P(),
            P("inner", None),
        ),
        out_specs=rows,
        check_vma=False,
    )
```

time: 385 us -> 164 us (0.43)
  waiting for transfers between devices: 295 us -> 0 us
  Pallas kernels: 0 us -> 154 us
  blocking collectives: 42.1 us -> 0 us
  matrix products: 26.5 us -> 0 us
  between operations: 13.2 us -> 0.15 us
  local copies, waits for them, and re-layouts: 1.22 us -> 6.39 us
    reduce_scatter x3 -> x0, waiting for transfers between devices: 214 us -> none  [the longest x2 142 us: dense_layer(): lax.psum_scatter(share, 'inner', scatter_dimension=0, tiled=True)]
    pallas_call x0 -> x3, Pallas kernels: none -> 154 us  [the longest x2 113 us: routed_layer(): pl.pallas_call(functools.partial(layer_kernel, devices), out_shape=jax.Sh...]
    all_gather x2 -> x0, waiting for transfers between devices: 79.8 us -> none  [dense_layer(): everyone = lax.all_gather(rows, 'inner', axis=0, tiled=True)]
    dot_general x5 -> x0, matrix products: 26.5 us -> none  [the longest x2 15.1 us: dense_layer(): projected = jnp.dot(everyone, gate_up, preferred_element_type=jnp.float32)]
    all_gather x1 -> x0, blocking collectives: 24.3 us -> none  [local(): both = lax.all_gather(both, 'inner', axis=0, tiled=True)]
    all_to_all x1 -> x0, blocking collectives: 17.8 us -> none  [local(): lax.all_to_all(merged_in, 'inner', split_axis=1, concat_axis=0, tiled=True)]
  transfers between devices with their start and end apart: 5 -> 0, of which waited for: 5 -> 0; matrix products, arithmetic and copies ran while one was open for 0% -> 0% of each run, Pallas kernels for 0% -> 0%
where the time goes in v1:
time: 164 us
  Pallas kernels  154 us (94%)
  local copies, waits for them, and re-layouts  6.39 us (4%)
  other arithmetic  3.26 us (2%)
    pallas_call x2, Pallas kernels, routed_layer(): pl.pallas_call(functools.partial(layer_kernel, devices), out_shape=jax.Sh...  113 us
    pallas_call x1, Pallas kernels, merge(): pl.pallas_call(functools.partial(merge_kernel, devices), out_shape=jax.Sh...  40.7 us
    concatenate x2, local copies, waits for them, and re-layouts, routed_layer(): jnp.concatenate([rows, high, low, jnp.zeros((tok, pad), jnp.bfloat16)], a...  3.49 us

profile of v1, /device:TPU:0, one launch (start us, length us, event | category | flops | bytes accessed | tf_op | source)
XLA Modules:
  0.0 164.0 jit_solution(16264263395243172167)
XLA Ops:
  0.0 0.0 copy-start
  0.0 0.0 copy-start.1
  0.0 0.0 copy-start.2
  0.0 0.8 select_reduce_fusion.1
  0.8 0.1 copy.30
  0.9 0.1 copy.29
  1.0 1.7 %concatenate.9.x_ref = bf16[64,2176]{1,0:T(8,128)(2,1)} concatenate(bf16[64,2048]{1,0:T(8,128)(2,1)} %param.13, bf16[64,16]{1,0:T(8,128)(2,1)S(1)} %copy.30, bf16[64,16]{1,0:T(8,128)(2,1)S(1)} %subtract_convert_fusion.1, bf16[64,96]{1,0:T(8,128)(2,1)S(1)} %broadcast.37), dimensions={1} | concatenate | bytes 557056 | tf_op jit(solution)/shard_map/concatenate | solution.py:304
  2.7 58.7 %shard_map.127.rows_ref = bf16[64,2048]{1,0:T(8,128)(2,1)} custom-call(bf16[64,2176]{1,0:T(8,128)(2,1)} %concatenate.9.x_ref, bf16[1,2048,1024]{2,1,0:T(8,128)(2,1)} %gu_ref.2, bf16[1,512,2048]{2,1,0:T(8,128)(2,1)} %down_ref.2), custom_call_target="tpu_custom_call" | custom-call | tf_op jit(solution)/shard_map/pallas_call | solution.py:307
  61.5 0.0 copy-start.3
  61.5 0.0 copy-start.4
  61.5 1.1 fusion
  62.6 0.0 copy-done
  62.6 0.2 fusion.3
  62.8 0.0 copy-done.1
  62.8 0.0 copy-done.2
  62.8 1.1 fusion.2
  64.0 0.8 copy.37
  64.9 40.7 %shard_map.128 = bf16[64,2048]{1,0:T(8,128)(2,1)} custom-call(bf16[16,64,256]{2,1,0:T(8,128)(2,1)} %bitcast.8, bf16[64,2048]{1,0:T(8,128)(2,1)} %shard_map.127.rows_ref, bf16[256,2048]{1,0:T(8,128)(2,1)} %weight_ref.1), custom_call_target="tpu_custom_call" | custom-call | tf_op jit(solution)/shard_map/pallas_call | solution.py:405
  105.6 0.0 copy-done.3
  105.6 0.0 copy-done.4
  105.7 0.1 copy.34
  105.8 0.1 copy.33
  105.9 1.7 %concatenate.11.x_ref = bf16[64,2176]{1,0:T(8,128)(2,1)} concatenate(bf16[64,2048]{1,0:T(8,128)(2,1)} %shard_map.128, bf16[64,16]{1,0:T(8,128)(2,1)S(1)} %copy.34, bf16[64,16]{1,0:T(8,128)(2,1)S(1)} %subtract_convert_fusion, bf16[64,96]{1,0:T(8,128)(2,1)S(1)} %broadcast.37), dimensions={1} | concatenate | bytes 557056 | tf_op jit(solution)/shard_map/concatenate | solution.py:304
  107.6 54.7 %shard_map.129 = bf16[64,2048]{1,0:T(8,128)(2,1)} custom-call(bf16[64,2176]{1,0:T(8,128)(2,1)} %concatenate.11.x_ref, bf16[1,2048,1024]{2,1,0:T(8,128)(2,1)} %gu_ref.3, bf16[1,512,2048]{2,1,0:T(8,128)(2,1)} %down_ref.3), custom_call_target="tpu_custom_call" | custom-call | tf_op jit(solution)/shard_map/pallas_call | solution.py:307
  162.3 1.7 %copy.39 = bf16[64,2048]{1,0:T(8,128)(2,1)} copy(bf16[64,2048]{1,0:T(8,128)(2,1)} %shard_map.129) | data formatting | bytes 524288
  (9 shorter events, 0.1 us)
Async XLA Ops:
  0.0 62.6 %copy-start = (bf16[64,2048]{1,0:T(8,128)(2,1)S(1)}, bf16[64,2048]{1,0:T(8,128)(2,1)}, u32[]{:S(2)}) copy-start(bf16[64,2048]{1,0:T(8,128)(2,1)} %param.14) | copy-start | bytes 786436
  0.0 62.8 %copy-start.1 = (f32[2048]{0:T(1024)S(1)}, f32[2048]{0:T(1024)}, u32[]{:S(2)}) copy-start(f32[2048]{0:T(1024)} %param.23) | copy-start | bytes 24580
  0.0 62.8 %copy-start.2 = (f32[2048]{0:T(1024)S(1)}, f32[2048]{0:T(1024)}, u32[]{:S(2)}) copy-start(f32[2048]{0:T(1024)} %param.24) | copy-start | bytes 24580
  61.5 44.1 %copy-start.3 = (f32[64,8]{0,1:T(8,128)S(1)}, f32[64,8]{0,1:T(8,128)}, u32[]{:S(2)}) copy-start(f32[64,8]{0,1:T(8,128)} %param.20) | copy-start | bytes 6148
  61.5 44.1 %copy-start.4 = (s32[64,8]{0,1:T(8,128)S(1)}, s32[64,8]{0,1:T(8,128)}, u32[]{:S(2)}) copy-start(s32[64,8]{0,1:T(8,128)} %param.19) | copy-start | bytes 6148

commit v2 on v0

v2 whole, which is shorter than its diff:
```python
import functools

import jax
import jax.numpy as jnp
from jax import lax
from jax.experimental import pallas as pl
from jax.experimental.pallas import tpu as pltpu
from jax.sharding import PartitionSpec as P

EPSILON = 1e-06
LANES = 128
PARTS = 2
LAG = 5
VMEM_LIMIT = 60 * 1024 * 1024


class Ring:
    def __init__(self, devices, tok):
        self.devices, self.tok = devices, tok
        self.chips = devices // 2
        self.reach = self.chips // 2
        self.rise = self.chips // 2
        me = lax.axis_index("inner")
        chip = me // 2
        across = chip % 2
        along = chip // 2
        self.core = me % 2
        self.place = along * (1 - across) + (2 * self.rise - 1 - along) * across
        self.me = me

    def device(self, shift, other):
        place = (self.place + shift + self.chips) % self.chips
        across = place // self.rise
        along = place * (1 - across) + (2 * self.rise - 1 - place) * across
        core = self.core * (1 - other) + (1 - self.core) * other
        return (along * 2 + across) * 2 + core

    def row(self, way, distance, other):
        if distance == 0:
            return ((self.reach - 1) * 4 + 2 + other) * self.tok
        if distance == self.reach:
            return ((self.reach - 1) * 4 + other) * self.tok
        return ((distance - 1) * 4 + way * 2 + other) * self.tok

    def half(self, way, distance, other, k):
        part = self.tok // 2
        return pl.ds(self.row(way, distance, other) + k * part, part)

    def block(self, way, distance, other):
        return pl.ds(self.row(way, distance, other), self.tok)


def remote(src, dst, send, recv, device):
    return pltpu.make_async_remote_copy(
        src_ref=src, dst_ref=dst, send_sem=send, recv_sem=recv,
        device_id={"inner": device}, device_id_type=pl.DeviceIdType.MESH,
    )


def greet(devices):
    barrier = pltpu.get_barrier_semaphore()
    for device in devices:
        pl.semaphore_signal(
            barrier, inc=1, device_id={"inner": device}, device_id_type=pl.DeviceIdType.MESH
        )
    pl.semaphore_wait(barrier, len(devices))


def wide(values):
    return values.astype(jnp.float32)


def narrow(values):
    return values.astype(jnp.bfloat16)


class Reduce:
    def __init__(self, ring, bufs, part):
        share, paired, arrived, pair_send, pair_recv, send, recv = bufs
        self.ring, self.part = ring, part
        self.share, self.paired, self.arrived = share.at[part], paired.at[part], arrived.at[part]
        self.pair_send, self.pair_recv, self.send, self.recv = pair_send, pair_recv, send, recv
        self.started = []

    def slots(self, distance):
        return (0,) if distance in (0, self.ring.reach) else (0, 1)

    def pair_copy(self, way, distance):
        ring = self.ring
        slot = ring.reach * 2 if distance == 0 else (distance - 1) * 2 + way
        here = self.paired.at[pl.ds(slot * ring.tok, ring.tok)]
        return remote(
            self.share.at[ring.block(way, distance, 1)], here,
            self.pair_send.at[self.part, slot], self.pair_recv.at[self.part, slot],
            ring.device(0, 1),
        ), here

    def start_pair(self, distance):
        for way in self.slots(distance):
            copy, _ = self.pair_copy(way, distance)
            copy.start()
            self.started.append(copy)

    def finish_pair(self, distance):
        for way in self.slots(distance):
            copy, here = self.pair_copy(way, distance)
            copy.wait_recv()
            rows = self.ring.block(way, distance, 0)
            self.share[rows, :] = narrow(wide(self.share[rows, :]) + wide(here[...]))

    def hop(self, way, distance, k):
        ring = self.ring
        rows = ring.tok // 2
        slot = (way * ring.reach + distance - 1) * 2 + k
        landing = self.arrived.at[pl.ds(slot * rows, rows)]
        return remote(
            self.share.at[ring.half(1 - way, distance, 0, k)], landing,
            self.send.at[self.part, slot], self.recv.at[self.part, slot],
            ring.device(1 - 2 * way, 0),
        ), landing

    def start_hop(self, way, distance, k):
        copy, _ = self.hop(way, distance, k)
        copy.start()
        self.started.append(copy)

    def step(self, way, distance, k):
        copy, landing = self.hop(way, distance + 1, k)
        copy.wait_recv()
        rows = self.ring.half(1 - way, distance, 0, k)
        self.share[rows, :] = narrow(wide(self.share[rows, :]) + wide(landing[...]))
        self.start_hop(way, distance, k)

    def early(self):
        reach = self.ring.reach
        if reach > 1:
            for way in (0, 1):
                self.start_hop(way, reach - 1, 1 - way)

    def late(self):
        for way in (0, 1):
            self.start_hop(way, self.ring.reach, way)

    def run(self):
        reach = self.ring.reach
        for distance in range(reach - 1, 0, -1):
            yield
            for way in (0, 1):
                self.step(way, distance, way)
            if distance > 1:
                for way in (0, 1):
                    self.step(way, distance - 1, 1 - way)
        yield
        totals = []
        for k in (0, 1):
            total = wide(self.share[self.ring.half(0, 0, 0, k), :])
            for way in (0, 1):
                if k == way or reach > 1:
                    copy, landing = self.hop(way, 1, k)
                    copy.wait_recv()
                    total = total + wide(landing[...])
            totals.append(total)
        return jnp.concatenate(totals, axis=0)


def reduce_scratch(devices, tok, width):
    reach = devices // 4
    return [
        pltpu.VMEM((PARTS, devices * tok, width), jnp.bfloat16),
        pltpu.VMEM((PARTS, (2 * reach + 1) * tok, width), jnp.bfloat16),
        pltpu.VMEM((PARTS, 2 * reach * tok, width), jnp.bfloat16),
        pltpu.SemaphoreType.DMA((PARTS, 2 * reach + 1)),
        pltpu.SemaphoreType.DMA((PARTS, 2 * reach + 1)),
        pltpu.SemaphoreType.DMA((PARTS, 4 * reach)),
        pltpu.SemaphoreType.DMA((PARTS, 4 * reach)),
    ]


def gather_scratch(devices, tok, width):
    reach = devices // 4
    return [
        pltpu.VMEM((PARTS, devices * tok, width), jnp.bfloat16),
        pltpu.SemaphoreType.DMA((PARTS, 4 * reach)),
        pltpu.SemaphoreType.DMA((PARTS, 4 * reach)),
        pltpu.SemaphoreType.DMA((PARTS, 4 * reach + 1)),
        pltpu.SemaphoreType.DMA((PARTS, 4 * reach + 1)),
    ]


def normed(values, gain):
    widened = wide(values)
    inverse_rms = lax.rsqrt(jnp.mean(widened * widened, axis=-1, keepdims=True) + EPSILON)
    return narrow(widened * inverse_rms * gain)


def gate_lanes(devices, lanes, tables):
    rows = tables[0][0].shape[0]
    lane = lax.broadcasted_iota(jnp.int32, (rows, lanes), 1)
    packed = jnp.zeros((rows, lanes), jnp.float32)
    for layer, (routes, gates) in enumerate(tables):
        base = 2 * layer * devices
        high_part = (lane >= base) & (lane < base + devices)
        low_part = (lane >= base + devices) & (lane < base + 2 * devices)
        expert = jnp.where(high_part, lane - base, lane - base - devices)
        dense = jnp.zeros((rows, lanes), jnp.float32)
        for k in range(routes.shape[1]):
            dense = dense + jnp.where(expert == routes[:, k : k + 1], gates[:, k : k + 1], 0.0)
        high = wide(narrow(dense))
        packed = jnp.where(high_part, high, jnp.where(low_part, dense - high, packed))
    return narrow(packed)


def block_kernel(devices, *refs):
    (hidden_ref, embed_ref, routes1, gates1, routes2, gates2, hidden_gain, embed_gain,
     gu1_ref, down1_ref, weight_ref, gu2_ref, down2_ref, out_ref) = refs[:14]
    scratch = list(refs[14:])
    take = lambda count: [scratch.pop(0) for _ in range(count)]
    gu1, down1, weight, gu2, down2, load_sem = take(6)
    packed, after_first, after_merge, pieces, columns, inner = take(6)
    piece_send, piece_recv, own_sem = take(3)
    gather1, gather2 = take(5), take(5)
    reduce1, reduce2, reduce3 = take(7), take(7), take(7)
    rows_all, width = hidden_ref.shape
    tok = rows_all // PARTS
    hidden = down1.shape[0]
    depth = weight.shape[0]
    lanes = packed.shape[1] - width
    ring = Ring(devices, tok)
    reach = ring.reach

    loads = [
        pltpu.make_async_copy(source, target, load_sem.at[i])
        for i, (source, target) in enumerate(
            [(gu1_ref.at[0], gu1), (down1_ref.at[0], down1), (weight_ref, weight),
             (gu2_ref.at[0], gu2), (down2_ref.at[0], down2)]
        )
    ]
    for load in loads:
        load.start()
    waiting = list(range(5))

    def need(*which):
        for i in which:
            if i in waiting:
                waiting.remove(i)
                loads[i].wait()

    packed[:, :width] = hidden_ref[...]
    packed[:, width:] = gate_lanes(
        devices, lanes, [(routes1[...], gates1[...]), (routes2[...], gates2[...])]
    )

    partners = [(0, 0, 1)]
    for distance in range(1, reach + 1):
        for other in (0, 1):
            partners.append((0, distance, other))
            if distance < reach:
                partners.append((1, distance, other))

    def target_of(way, distance, other):
        return ring.device(distance * (1 - 2 * way), other)

    greet([target_of(*partner) for partner in partners])
    started = []

    def begin(copy):
        copy.start()
        started.append(copy)

    def layer(part, source, bufs, first, reduce_bufs, load_ids, gu, down):
        everyone, send, recv, sib_send, sib_recv = bufs
        everyone = everyone.at[part]
        own_rows = pl.ds(part * tok, tok)

        def ring_copy(way, distance, k):
            slot = (way * reach + distance - 1) * 2 + k
            landing = everyone.at[ring.half(way, distance, 0, k)]
            origin = (
                source.at[pl.ds(part * tok + k * (tok // 2), tok // 2)]
                if distance == 1
                else everyone.at[ring.half(way, distance - 1, 0, k)]
            )
            return remote(
                origin, landing, send.at[part, slot], recv.at[part, slot],
                ring.device(1 - 2 * way, 0),
            )

        def sibling_copy(way, distance, k):
            if distance == 0:
                slot, origin, landing = 4 * reach, source.at[own_rows], everyone.at[ring.block(0, 0, 1)]
            else:
                slot = (way * reach + distance - 1) * 2 + k
                origin = everyone.at[ring.half(way, distance, 0, k)]
                landing = everyone.at[ring.half(way, distance, 1, k)]
            return remote(
                origin, landing, sib_send.at[part, slot], sib_recv.at[part, slot],
                ring.device(0, 1),
            )

        reducing = Reduce(ring, reduce_bufs, part)
        share = reducing.share
        gate_rows = gather1[0].at[part]

        def compute(distance):
            rows = pl.ds((distance - 1) * 4 * tok, 4 * tok)
            x = everyone.at[rows]
            step = min(256, hidden)

            @pl.loop(0, hidden // step)
            def _(j):
                left = pl.ds(pl.multiple_of(j * step, step), step)
                right = pl.ds(pl.multiple_of(hidden + j * step, step), step)
                g = jnp.dot(x[:, :width], gu[:, left], preferred_element_type=jnp.float32)
                u = jnp.dot(x[:, :width], gu[:, right], preferred_element_type=jnp.float32)
                inner[:, left] = narrow(jax.nn.silu(g) * u)

            lane = lax.broadcasted_iota(jnp.int32, (4 * tok, lanes), 1)
            mine = (lane == ring.me + first * devices) | (lane == ring.me + (first + 1) * devices)
            gate = jnp.sum(
                jnp.where(mine, wide(gate_rows[rows, width:]), 0.0), axis=1, keepdims=True
            )
            span = min(512, width)

            @pl.loop(0, width // span)
            def _(j):
                part_columns = pl.ds(pl.multiple_of(j * span, span), span)
                out = jnp.dot(inner[...], down[:, part_columns], preferred_element_type=jnp.float32)
                share[rows, part_columns] = narrow(out * gate)

        def streams(distance):
            for short in (0, 1):
                if not (short and distance == reach):
                    for way in (0, 1):
                        yield way, (1 - way if short else way), short

        for way, k, _ in streams(1):
            begin(ring_copy(way, 1, k))
        begin(sibling_copy(0, 0, 0))
        everyone[ring.block(0, 0, 0), :] = source[own_rows, :]
        for distance in range(1, reach + 1):
            yield
            for way, k, short in streams(distance):
                ring_copy(way, distance, k).wait_recv()
                if distance < reach and not (short and distance == reach - 1):
                    begin(ring_copy(way, distance + 1, k))
                begin(sibling_copy(way, distance, k))
            if distance == 1:
                need(*load_ids)
            else:
                for way, k, _ in streams(distance - 1):
                    sibling_copy(way, distance - 1, k).wait_recv()
                compute(distance - 1)
                reducing.start_pair(distance - 1)
        for distance in range(1, reach):
            reducing.finish_pair(distance)
        reducing.early()
        yield
        for way, k, _ in streams(reach):
            sibling_copy(way, reach, k).wait_recv()
        sibling_copy(0, 0, 0).wait_recv()
        compute(reach)
        reducing.start_pair(reach)
        reducing.start_pair(0)
        reducing.finish_pair(reach)
        reducing.late()
        reducing.finish_pair(0)
        total = yield from reducing.run()
        started.extend(reducing.started)
        return total

    def merged(part):
        here, landed = pieces.at[part], columns.at[part]

        def piece(way, distance, other):
            target = target_of(way, distance, other)
            slot = ring.row(way, distance, other) // tok
            return remote(
                here.at[target], landed.at[ring.block(way, distance, other)],
                piece_send.at[part, slot], piece_recv.at[part, slot], target,
            )

        for partner in reversed(partners):
            begin(piece(*partner))
        own = pltpu.make_async_copy(
            here.at[ring.me], landed.at[ring.block(0, 0, 0)], own_sem.at[part]
        )
        own.start()
        need(2)
        reducing = Reduce(ring, reduce2, part)
        share = reducing.share
        for distance in range(reach, 0, -1):
            if distance % 2 == 0:
                yield
            if distance == reach:
                own.wait()
            for way, far, other in partners:
                if far == distance or (far == 0 and distance == reach):
                    piece(way, far, other).wait_recv()
            rows = pl.ds((distance - 1) * 4 * tok, 4 * tok)
            span = min(512, width)

            @pl.loop(0, width // span)
            def _(j):
                cut = pl.ds(pl.multiple_of(j * span, span), span)
                share[rows, cut] = narrow(
                    jnp.dot(landed[rows, :], weight[:, cut], preferred_element_type=jnp.float32)
                )

            reducing.start_pair(distance)
            if distance == reach:
                reducing.start_pair(0)
                reducing.finish_pair(reach)
                reducing.late()
                reducing.finish_pair(0)
            else:
                reducing.finish_pair(distance)
                if distance == reach - 1:
                    reducing.early()
        total = yield from reducing.run()
        started.extend(reducing.started)
        return total

    def scatter_pieces(part, values, at):
        for j in range(width // depth):
            pieces[part, at + j] = values[:, j * depth : (j + 1) * depth]

    def pipeline(part):
        rows = pl.ds(part * tok, tok)
        total = yield from layer(part, packed, gather1, 0, reduce1, (0, 1), gu1, down1)
        first = narrow(wide(hidden_ref[rows, :]) + total)
        after_first[rows, :] = first
        scatter_pieces(part, normed(first, hidden_gain[...]), 0)
        total = yield from merged(part)
        after_merge[rows, :] = narrow(wide(after_first[rows, :]) + jax.nn.silu(total))
        total = yield from layer(part, after_merge, gather2, 2, reduce3, (3, 4), gu2, down2)
        out_ref[rows, :] = narrow(wide(after_merge[rows, :]) + total)

    lines = [pipeline(part) for part in range(PARTS)]
    done = object()
    tick = 0
    while lines:
        for at, line in enumerate(list(lines)):
            if tick >= at * LAG or len(lines) < PARTS:
                if next(line, done) is done:
                    lines.remove(line)
        if tick == 0:
            for part in range(PARTS):
                rows = pl.ds(part * tok, tok)
                scatter_pieces(part, normed(embed_ref[rows, :], embed_gain[...]), width // depth)
        tick += 1
    for copy in started:
        copy.wait_send()


def fused(hidden_rows, token_embed, first_routes, first_gates, first_gate_up, first_down,
          second_routes, second_gates, second_gate_up, second_down, hidden_gain, embed_gain,
          merge_weight):
    devices = lax.axis_size("inner")
    rows, width = hidden_rows.shape
    tok = rows // PARTS
    hidden = first_down.shape[1]
    depth = merge_weight.shape[0]
    lanes = -(-4 * devices // LANES) * LANES
    vmem = pl.BlockSpec(memory_space=pltpu.VMEM)
    hbm = pl.BlockSpec(memory_space=pl.ANY)
    bf16 = jnp.bfloat16
    scratch = [
        pltpu.VMEM(first_gate_up.shape[1:], bf16),
        pltpu.VMEM(first_down.shape[1:], bf16),
        pltpu.VMEM(merge_weight.shape, bf16),
        pltpu.VMEM(second_gate_up.shape[1:], bf16),
        pltpu.VMEM(second_down.shape[1:], bf16),
        pltpu.SemaphoreType.DMA((5,)),
        pltpu.VMEM((rows, width + lanes), bf16),
        pltpu.VMEM((rows, width), bf16),
        pltpu.VMEM((rows, width), bf16),
        pltpu.VMEM((PARTS, devices, tok, depth), bf16),
        pltpu.VMEM((PARTS, devices * tok, depth), bf16),
        pltpu.VMEM((4 * tok, hidden), bf16),
        pltpu.SemaphoreType.DMA((PARTS, devices)),
        pltpu.SemaphoreType.DMA((PARTS, devices)),
        pltpu.SemaphoreType.DMA((PARTS,)),
    ]
    scratch += gather_scratch(devices, tok, width + lanes) + gather_scratch(devices, tok, width)
    for _ in range(3):
        scratch += reduce_scratch(devices, tok, width)
    return pl.pallas_call(
        functools.partial(block_kernel, devices),
        out_shape=jax.ShapeDtypeStruct((rows, width), bf16),
        in_specs=[vmem] * 8 + [hbm] * 5,
        out_specs=vmem,
        scratch_shapes=scratch,
        compiler_params=pltpu.CompilerParams(
            collective_id=0, has_side_effects=True, vmem_limit_bytes=VMEM_LIMIT
        ),
    )(hidden_rows, token_embed, first_routes, first_gates, second_routes, second_gates,
      hidden_gain[None], embed_gain[None], first_gate_up, first_down, merge_weight,
      second_gate_up, second_down)


def rms_scale(values, gain_vec):
    widened = values.astype(jnp.float32)
    inverse_rms = lax.rsqrt(jnp.mean(widened * widened, axis=-1, keepdims=True) + EPSILON)
    return (widened * inverse_rms * gain_vec).astype(jnp.bfloat16)


def dense_gates(routes, gates, experts):
    hit = routes[:, :, None] == jnp.arange(experts, dtype=jnp.int32)[None, None, :]
    return jnp.sum(jnp.where(hit, gates[:, :, None], 0.0), axis=1)


def plain_layer(devices, rows, routes, gates, gate_up, down):
    dense = lax.all_gather(dense_gates(routes, gates, devices), "inner", axis=0, tiled=True)
    column = lax.dynamic_slice_in_dim(dense, lax.axis_index("inner"), 1, axis=1)
    everyone = lax.all_gather(rows, "inner", axis=0, tiled=True)
    width = down.shape[1]
    projected = jnp.dot(everyone, gate_up[0], preferred_element_type=jnp.float32)
    inner = narrow(jax.nn.silu(projected[:, :width]) * projected[:, width:])
    share = narrow(jnp.dot(inner, down[0], preferred_element_type=jnp.float32) * column)
    total = lax.psum_scatter(share, "inner", scatter_dimension=0, tiled=True)
    return narrow(wide(rows) + wide(total))


def plain_merge(after_first, merged_in, weight):
    columns = lax.all_to_all(merged_in, "inner", split_axis=1, concat_axis=0, tiled=True)
    partial = narrow(jnp.dot(columns, weight, preferred_element_type=jnp.float32))
    merged = lax.psum_scatter(partial, "inner", scatter_dimension=0, tiled=True)
    return narrow(wide(after_first) + jax.nn.silu(wide(merged)))


def unfused(hidden_rows, token_embed, first_routes, first_gates, first_gate_up, first_down,
            second_routes, second_gates, second_gate_up, second_down, hidden_gain, embed_gain,
            merge_weight):
    devices = lax.axis_size("inner")
    after_first = plain_layer(
        devices, hidden_rows, first_routes, first_gates, first_gate_up, first_down
    )
    merged_in = jnp.concatenate(
        [rms_scale(after_first, hidden_gain), rms_scale(token_embed, embed_gain)], axis=1
    )
    after_merge = plain_merge(after_first, merged_in, merge_weight)
    return plain_layer(devices, after_merge, second_routes, second_gates, second_gate_up, second_down)


def local(hidden_rows, *others):
    devices = lax.axis_size("inner")
    tok, width = hidden_rows.shape
    fits = 12 * devices * tok * width * 2 <= VMEM_LIMIT and devices % 4 == 0 and tok % 32 == 0
    return (fused if fits else unfused)(hidden_rows, *others)


def solution(mesh):
    rows = P(("groups", "inner"), None)
    return jax.shard_map(
        local,
        mesh=mesh,
        in_specs=(
            rows, rows, rows, rows,
            P("inner", None, None),
            P("inner", None, None),
            rows, rows,
            P("inner", None, None),
            P("inner", None, None),
            P(),
            P(),
            P("inner", None),
        ),
        out_specs=rows,
        check_vma=False,
    )
```

time: 385 us -> 167 us (0.43)
  waiting for transfers between devices: 295 us -> 0 us
  Pallas kernels: 0 us -> 160 us
  blocking collectives: 42.1 us -> 0 us
  matrix products: 26.5 us -> 0 us
  between operations: 13.2 us -> 0.01 us
  other arithmetic: 7.03 us -> 0 us
  local copies, waits for them, and re-layouts: 1.22 us -> 7.17 us
    reduce_scatter x3 -> x0, waiting for transfers between devices: 214 us -> none  [the longest x2 142 us: dense_layer(): lax.psum_scatter(share, 'inner', scatter_dimension=0, tiled=True)]
    pallas_call x0 -> x1, Pallas kernels: none -> 160 us  [fused(): pl.pallas_call(functools.partial(block_kernel, devices), out_shape=jax.Sh...]
    all_gather x2 -> x0, waiting for transfers between devices: 79.8 us -> none  [dense_layer(): everyone = lax.all_gather(rows, 'inner', axis=0, tiled=True)]
    dot_general x5 -> x0, matrix products: 26.5 us -> none  [the longest x2 15.1 us: dense_layer(): projected = jnp.dot(everyone, gate_up, preferred_element_type=jnp.float32)]
    all_gather x1 -> x0, blocking collectives: 24.3 us -> none  [local(): both = lax.all_gather(both, 'inner', axis=0, tiled=True)]
    all_to_all x1 -> x0, blocking collectives: 17.8 us -> none  [local(): lax.all_to_all(merged_in, 'inner', split_axis=1, concat_axis=0, tiled=True)]
    unnamed x19 -> x5, local copies, waits for them, and re-layouts: 1.02 us -> 7.17 us
    convert_element_type x4 -> x0, other arithmetic: 4.79 us -> none  [the longest x1 1.85 us: local(): (after_first.astype(jnp.float32) + jax.nn.silu(merged)).astype(jnp.bfloat16)]
  transfers between devices with their start and end apart: 5 -> 0, of which waited for: 5 -> 0; matrix products, arithmetic and copies ran while one was open for 0% -> 0% of each run, Pallas kernels for 0% -> 0%
where the time goes in v2:
time: 167 us
  Pallas kernels  160 us (96%)
  local copies, waits for them, and re-layouts  7.17 us (4%)
    pallas_call x1, Pallas kernels, fused(): pl.pallas_call(functools.partial(block_kernel, devices), out_shape=jax.Sh...  160 us
    unnamed x5, local copies, waits for them, and re-layouts  7.17 us

profile of v2, /device:TPU:0, one launch (start us, length us, event | category | flops | bytes accessed | tf_op | source)
XLA Modules:
  0.0 166.7 jit_solution(14553778166332885797)
XLA Ops:
  0.0 1.4 copy.14.refs_2_
  1.4 1.4 copy.15.refs_3_
  2.8 1.4 copy.16.refs_4_
  4.1 1.4 copy.17.refs_5_
  5.5 159.5 %shard_map.127 = bf16[64,2048]{1,0:T(8,128)(2,1)} custom-call(bf16[64,2048]{1,0:T(8,128)(2,1)} %refs_0_.1, bf16[64,2048]{1,0:T(8,128)(2,1)} %refs_1_.1, s32[64,8]{1,0:T(8,128)} %copy.14.refs_2_, f32[64,8]{1,0:T(8,128)} %copy.15.refs_3_, s32[64,8]{1,0:T(8,128)} %copy.16.refs_4_, f32[64,8]{1,0:T(8,128)} %copy.17.refs_5_, f32[1,2048]{1,0:T(1,128)} %bitcast.2, ...), custom_call_target="tpu_custom_call" | custom-call | tf_op jit(solution)/shard_map/pallas_call | solution.py:487
  165.0 1.7 %copy.19 = bf16[64,2048]{1,0:T(8,128)(2,1)} copy(bf16[64,2048]{1,0:T(8,128)(2,1)} %shard_map.127) | data formatting | bytes 524288

commit v3 on v2

--- a/solution.py
+++ b/solution.py
@@ -9,8 +9,8 @@
 
 EPSILON = 1e-06
 LANES = 128
-PARTS = 2
-LAG = 5
+PARTS = 1
+LAG = 0
 VMEM_LIMIT = 60 * 1024 * 1024
 
 
@@ -301,20 +301,29 @@
         share = reducing.share
         gate_rows = gather1[0].at[part]
 
-        def compute(distance):
-            rows = pl.ds((distance - 1) * 4 * tok, 4 * tok)
-            x = everyone.at[rows]
+        def span_of(distance):
+            if distance == 0:
+                return ring.row(0, 0, 0), 2 * tok
+            return (distance - 1) * 4 * tok, (2 if distance == reach else 4) * tok
+
+        def up(distance):
+            first_row, count = span_of(distance)
+            rows = pl.ds(first_row, count)
             step = min(256, hidden)
 
             @pl.loop(0, hidden // step)
             def _(j):
                 left = pl.ds(pl.multiple_of(j * step, step), step)
                 right = pl.ds(pl.multiple_of(hidden + j * step, step), step)
-                g = jnp.dot(x[:, :width], gu[:, left], preferred_element_type=jnp.float32)
-                u = jnp.dot(x[:, :width], gu[:, right], preferred_element_type=jnp.float32)
-                inner[:, left] = narrow(jax.nn.silu(g) * u)
-
-            lane = lax.broadcasted_iota(jnp.int32, (4 * tok, lanes), 1)
+                x = everyone[rows, :width]
+                g = jnp.dot(x, gu[:, left], preferred_element_type=jnp.float32)
+                u = jnp.dot(x, gu[:, right], preferred_element_type=jnp.float32)
+                inner[part, :count, left] = narrow(jax.nn.silu(g) * u)
+
+        def finish(distance):
+            first_row, count = span_of(distance)
+            rows = pl.ds(first_row, count)
+            lane = lax.broadcasted_iota(jnp.int32, (count, lanes), 1)
             mine = (lane == ring.me + first * devices) | (lane == ring.me + (first + 1) * devices)
             gate = jnp.sum(
                 jnp.where(mine, wide(gate_rows[rows, width:]), 0.0), axis=1, keepdims=True
@@ -323,9 +332,13 @@
 
             @pl.loop(0, width // span)
             def _(j):
-                part_columns = pl.ds(pl.multiple_of(j * span, span), span)
-                out = jnp.dot(inner[...], down[:, part_columns], preferred_element_type=jnp.float32)
-                share[rows, part_columns] = narrow(out * gate)
+                cut = pl.ds(pl.multiple_of(j * span, span), span)
+                out = jnp.dot(
+                    inner[part, :count, :], down[:, cut], preferred_element_type=jnp.float32
+                )
+                share[rows, cut] = narrow(out * gate)
+
+            reducing.start_pair(distance)
 
         def streams(distance):
             for short in (0, 1):
@@ -337,33 +350,58 @@
             begin(ring_copy(way, 1, k))
         begin(sibling_copy(0, 0, 0))
         everyone[ring.block(0, 0, 0), :] = source[own_rows, :]
-        for distance in range(1, reach + 1):
+
+        def pass_on(distance, short):
+            for way, k, which in streams(distance):
+                if which == short:
+                    ring_copy(way, distance, k).wait_recv()
+                    if distance < reach and not (short and distance == reach - 1):
+                        begin(ring_copy(way, distance + 1, k))
+                    begin(sibling_copy(way, distance, k))
+
+        def from_sibling(distance):
+            if distance == 0:
+                sibling_copy(0, 0, 0).wait_recv()
+            else:
+                for way, k, _ in streams(distance):
+                    sibling_copy(way, distance, k).wait_recv()
+
+        yield
+        need(*load_ids)
+        from_sibling(0)
+        up(0)
+        for distance in range(1, reach):
             yield
-            for way, k, short in streams(distance):
-                ring_copy(way, distance, k).wait_recv()
-                if distance < reach and not (short and distance == reach - 1):
-                    begin(ring_copy(way, distance + 1, k))
-                begin(sibling_copy(way, distance, k))
+            pass_on(distance, 0)
             if distance == 1:
-                need(*load_ids)
+                finish(0)
             else:
-                for way, k, _ in streams(distance - 1):
-                    sibling_copy(way, distance - 1, k).wait_recv()
-                compute(distance - 1)
-                reducing.start_pair(distance - 1)
-        for distance in range(1, reach):
-            reducing.finish_pair(distance)
-        reducing.early()
+                from_sibling(distance - 1)
+                up(distance - 1)
+            yield
+            pass_on(distance, 1)
+            if distance > 1:
+                finish(distance - 1)
+                reducing.finish_pair(distance - 2)
         yield
-        for way, k, _ in streams(reach):
-            sibling_copy(way, reach, k).wait_recv()
-        sibling_copy(0, 0, 0).wait_recv()
-        compute(reach)
-        reducing.start_pair(reach)
-        reducing.start_pair(0)
+        if reach > 1:
+            from_sibling(reach - 1)
+            up(reach - 1)
+        yield
+        pass_on(reach, 0)
+        if reach > 1:
+            finish(reach - 1)
+            reducing.finish_pair(reach - 2)
+        yield
+        from_sibling(reach)
+        up(reach)
+        if reach > 1:
+            reducing.finish_pair(reach - 1)
+            reducing.early()
+        finish(reach)
+        yield
         reducing.finish_pair(reach)
         reducing.late()
-        reducing.finish_pair(0)
         total = yield from reducing.run()
         started.extend(reducing.started)
         return total
@@ -476,7 +514,7 @@
         pltpu.VMEM((rows, width), bf16),
         pltpu.VMEM((PARTS, devices, tok, depth), bf16),
         pltpu.VMEM((PARTS, devices * tok, depth), bf16),
-        pltpu.VMEM((4 * tok, hidden), bf16),
+        pltpu.VMEM((PARTS, 4 * tok, hidden), bf16),
         pltpu.SemaphoreType.DMA((PARTS, devices)),
         pltpu.SemaphoreType.DMA((PARTS, devices)),
         pltpu.SemaphoreType.DMA((PARTS,)),

time: 167 us -> 154 us (0.922)
  Pallas kernels: 160 us -> 146 us
    pallas_call x1, Pallas kernels: 160 us -> 146 us  [fused(): pl.pallas_call(functools.partial(block_kernel, devices), out_shape=jax.Sh...]
where the time goes in v3:
time: 154 us; the launch traced here: 153 us
  Pallas kernels  146 us (95%)
  local copies, waits for them, and re-layouts  7.17 us (5%)
    pallas_call x1, Pallas kernels, fused(): pl.pallas_call(functools.partial(block_kernel, devices), out_shape=jax.Sh...  146 us
    unnamed x5, local copies, waits for them, and re-layouts  7.17 us

profile of v3, /device:TPU:0, one launch (start us, length us, event | category | flops | bytes accessed | tf_op | source)
XLA Modules:
  0.0 153.4 jit_solution(2331287693861512776)
XLA Ops:
  0.0 1.4 copy.14.refs_2_
  1.4 1.4 copy.15.refs_3_
  2.8 1.4 copy.16.refs_4_
  4.1 1.4 copy.17.refs_5_
  5.5 146.3 %shard_map.127 = bf16[64,2048]{1,0:T(8,128)(2,1)} custom-call(bf16[64,2048]{1,0:T(8,128)(2,1)} %refs_0_.1, bf16[64,2048]{1,0:T(8,128)(2,1)} %refs_1_.1, s32[64,8]{1,0:T(8,128)} %copy.14.refs_2_, f32[64,8]{1,0:T(8,128)} %copy.15.refs_3_, s32[64,8]{1,0:T(8,128)} %copy.16.refs_4_, f32[64,8]{1,0:T(8,128)} %copy.17.refs_5_, f32[1,2048]{1,0:T(1,128)} %bitcast.2, ...), custom_call_target="tpu_custom_call" | custom-call | tf_op jit(solution)/shard_map/pallas_call | solution.py:525
  151.8 1.7 %copy.19 = bf16[64,2048]{1,0:T(8,128)(2,1)} copy(bf16[64,2048]{1,0:T(8,128)(2,1)} %shard_map.127) | data formatting | bytes 524288
